TPU v7x, 32 devices: a whole 2x2x4 slice. The times are simulated.
32 devices in a mesh: rep: 2 (over y), seq: 8 (over z, x), grp: 2 (over core).
Axes of the slice: x: 2, y: 2, z: 4, core: 2. Of those that a mesh axis runs over, the one named last changes fastest.
Arguments:
- hidden: bfloat16 [4352, 8192], P(('rep', 'seq'), 'grp'), parts along dimension 0, may hold values from -6 to 6
- proj: bfloat16 [3, 256, 8192], P(None, 'seq', 'grp'), may hold values from -0.0625 to 0.0625
- short_taps: float32 [3, 3, 256], P(None, None, 'grp'), may hold values from -4 to 4
- filters: float32 [16, 128], P('grp'), may hold values from -0.5 to 0.5
- grad_out: bfloat16 [4352, 256], P(('rep', 'seq'), 'grp'), parts along dimension 0, may hold values from -6 to 6
- var_pos: int32 [256], P(('rep', 'seq')), parts along dimension 0, may hold values from 0 to 2175, as said below
- alt_hidden: bfloat16 [256, 8192], P(('rep', 'seq'), 'grp'), parts along dimension 0, may hold values from -6 to 6
Outputs:
- attribution: float32 [4352], P(('rep', 'seq')), parts along dimension 0
- effect: float32 [256], P(('rep', 'seq')), parts along dimension 0
There are 2 independent parts, one for each index of `rep`. A program takes and returns all parts, laid end to end along the dimension named above; an argument that names none is the same for every part. Nothing has to cross between parts.
Inputs may be any that keep to these rules, and one draw needn't show every extreme that they name: `var_pos`: variants v of block j (j * 16 <= v < (j + 1) * 16) lie in tokens j * 272 to (j + 1) * 272 - 1; each block holds the first and the last of those tokens.
All inputs are finite; a program needn't handle non-finite values.
Results may differ from a plain program's by a relative error of at most 0.0028.
Values may be sent and summed in bfloat16 or wider, within the bound.
No kernel may reach another device: no remote copies, remote signals or barrier semaphores. Data moves between devices by JAX's collectives and lax.ppermute only.
A program may use at most 64 MiB of HBM per device.

v0:
```python
import jax
import jax.numpy as jnp
from jax import lax
from jax.sharding import PartitionSpec as P

D = 8192
GROUP = 16


def shifted(block, axis, distance):
    devices = range(lax.axis_size(axis))
    route = [(i - distance, i) for i in devices if i - distance in devices]
    return lax.ppermute(block, axis, route)


def causal_taps(source, taps, leading):
    tap_count = taps.shape[0]
    row_count = source.shape[0]
    extended = jnp.concatenate([leading, source], 0)
    summed = jnp.zeros(source.shape, jnp.float32)
    for offset in range(tap_count):
        begin = tap_count - 1 - offset
        summed = summed + taps[offset] * extended[begin : begin + row_count]
    return summed


def later_taps(source, taps, trailing):
    tap_count = taps.shape[0]
    row_count = source.shape[0]
    extended = jnp.concatenate([source, trailing], 0)
    summed = jnp.zeros(source.shape, jnp.float32)
    for offset in range(tap_count):
        summed = summed + taps[offset] * extended[offset : offset + row_count]
    return summed


def long_filter(extended, filters, row_count, later):
    filter_span = filters.shape[1]
    per_channel = jnp.repeat(filters, GROUP, axis=0).T

    def accumulate(block, summed):
        for inner in range(8):
            offset = block * 8 + inner
            begin = offset if later else filter_span - 1 - offset
            section = lax.dynamic_slice_in_dim(extended, begin, row_count, 0)
            summed = (
                summed + lax.dynamic_index_in_dim(per_channel, offset, 0, keepdims=False) * section
            )
        return summed

    return lax.fori_loop(
        0, filter_span // 8, accumulate, jnp.zeros((row_count, extended.shape[1]), jnp.float32)
    )


def per_device(hidden, proj, short_taps, filters, grad_out, var_pos, alt_hidden):
    row_count = hidden.shape[0]
    tap_count = short_taps.shape[0]
    filter_span = filters.shape[1]
    partial_feature = jnp.einsum(
        "td,fcd->tfc",
        hidden,
        lax.all_gather(proj, "seq", axis=1, tiled=True),
        preferred_element_type=jnp.float32,
    )
    feature = lax.psum_scatter(partial_feature, "grp", scatter_dimension=2, tiled=True)
    short_rim = shifted(feature[row_count - tap_count + 1 :], "seq", 1)
    mixed = causal_taps(feature, short_taps, short_rim)
    product = mixed[:, 1] * mixed[:, 2]
    prior_product = shifted(product[row_count - filter_span + 1 :], "seq", 1)
    queries = mixed[:, 0]
    filtered = long_filter(jnp.concatenate([prior_product, product], 0), filters, row_count, False)
    upstream = grad_out.astype(jnp.float32)
    back_queries = upstream * filtered
    back_filtered = upstream * queries
    next_filtered = shifted(back_filtered[: filter_span - 1], "seq", -1)
    back_product = long_filter(
        jnp.concatenate([back_filtered, next_filtered], 0), filters, row_count, True
    )
    back_mixed = jnp.stack(
        [back_queries, back_product * mixed[:, 2], back_product * mixed[:, 1]], 1
    )
    next_mixed = shifted(back_mixed[: tap_count - 1], "seq", -1)
    back_feature = later_taps(back_mixed, short_taps, next_mixed).astype(jnp.bfloat16)
    all_channels = lax.all_gather(back_feature, "grp", axis=2, tiled=True)
    panels_again = lax.all_gather(proj, "seq", axis=1, tiled=True)
    back_hidden = jnp.einsum(
        "tfc,fcd->td", all_channels, panels_again, preferred_element_type=jnp.float32
    )
    hidden_float = hidden.astype(jnp.float32)
    attribution_part = jnp.sum(back_hidden * hidden_float, 1)
    local_rows = var_pos - lax.axis_index("seq") * row_count
    picked = jnp.take(back_hidden, local_rows, axis=0)
    present = jnp.take(hidden_float, local_rows, axis=0)
    change = alt_hidden.astype(jnp.float32) - present
    effect_part = jnp.sum(picked * change, 1)
    attribution, effect = lax.psum((attribution_part, effect_part), "grp")
    factor = D ** (-0.5)
    return (attribution * factor, effect * factor)


def solution(mesh):
    in_specs = (
        P(("rep", "seq"), "grp"),
        P(None, "seq", "grp"),
        P(None, None, "grp"),
        P("grp", None),
        P(("rep", "seq"), "grp"),
        P(("rep", "seq")),
        P(("rep", "seq"), "grp"),
    )
    out_specs = (P(("rep", "seq")), P(("rep", "seq")))
    return jax.shard_map(
        per_device, mesh=mesh, in_specs=in_specs, out_specs=out_specs, check_vma=False
    )
```

profile of v0, /device:TPU:9, one launch (start us, length us, event | category | flops | bytes accessed | tf_op | source)
XLA Modules:
  0.0 182.6 jit_solution(11757446988338695483)
XLA Ops:
  7.2 0.7 all-gather.2.cloned.1.call-update
  8.0 100.1 %all-gather.2.cloned.1.call-done = bf16[3,256,4096]{2,1,0:T(8,128)(2,1)} async-done(((bf16[3,32,4096]{2,1,0:T(8,128)(2,1)}), bf16[3,256,4096]{2,1,0:T(8,128)(2,1)}) %all-gather.2.cloned.1.call-update) | async-done | bytes 6291472 | tf_op jit(solution)/shard_map/all_gather | solution.py:63
  108.1 6.3 %fusion.30 = f32[272,3,256]{2,0,1:T(8,128)} fusion(bf16[3,256,4096]{2,1,0:T(8,128)(2,1)} %all-gather.2.cloned.1.call-done, bf16[272,4096]{1,0:T(8,128)(2,1)} %param.13), kind=kOutput, calls=%fused_computation.52 | convolution fusion | flops 1711276032 | bytes 9355264 | tf_op jit(solution)/shard_map/td,fcd->tfc/dot_general | solution.py:60
  114.5 9.7 %reduce-scatter.2.cloned.1.call-done = f32[272,3,128]{2,0,1:T(8,128)} async-done(((f32[272,3,256]{2,0,1:T(8,128)}), f32[272,3,128]{2,0,1:T(8,128)}) %reduce-scatter.2.cloned.1.call-update) | async-done | bytes 417808 | tf_op jit(solution)/shard_map/reduce_scatter | solution.py:66
  124.1 0.7 slice.65
  124.9 3.1 %collective-permute-start = (f32[2,3,128]{2,0,1:T(2,128)S(1)}, f32[2,3,128]{2,0,1:T(2,128)S(1)}, u32[]{:S(2)}, u32[]{:S(2)}) collective-permute-start(f32[2,3,128]{2,0,1:T(2,128)S(1)} %slice.65), channel_id=1, source_target_pairs={{0,2},{2,4},{4,6},{6,8},{8,10},{10,12},{12,14},{1,3},{3,5},{5,7},{... | collective-permute-start | bytes 9224 | tf_op jit(solution)/shard_map/ppermute | solution.py:13
  127.9 2.1 %collective-permute-done = f32[2,3,128]{2,0,1:T(2,128)S(1)} collective-permute-done((f32[2,3,128]{2,0,1:T(2,128)S(1)}, f32[2,3,128]{2,0,1:T(2,128)S(1)}, u32[]{:S(2)}, u32[]{:S(2)}) %collective-permute-start) | collective-permute-done | bytes 3104 | tf_op jit(solution)/shard_map/ppermute | solution.py:13
  130.1 1.5 fusion.35
  131.7 2.2 %collective-permute-start.2 = (f32[127,128]{1,0:T(8,128)S(1)}, f32[127,128]{1,0:T(8,128)S(1)}, u32[]{:S(2)}, u32[]{:S(2)}) collective-permute-start(f32[127,128]{1,0:T(8,128)S(1)} %slice.72), channel_id=1, source_target_pairs={{2,0},{4,2},{6,4},{8,6},{10,8},{12,10},{14,12},{3,1},{5,3},{7,5},{... | collective-permute-start | bytes 195080 | tf_op jit(solution)/shard_map/ppermute | solution.py:13
  134.0 3.1 %collective-permute-start.1 = (f32[127,128]{1,0:T(8,128)S(1)}, f32[127,128]{1,0:T(8,128)S(1)}, u32[]{:S(2)}, u32[]{:S(2)}) collective-permute-start(f32[127,128]{1,0:T(8,128)S(1)} %slice.70), channel_id=1, source_target_pairs={{0,2},{2,4},{4,6},{6,8},{8,10},{10,12},{12,14},{1,3},{3,5},{5,7},{... | collective-permute-start | bytes 195080 | tf_op jit(solution)/shard_map/ppermute | solution.py:13
  137.2 5.7 %while.34 = (s32[]{:T(128)}, f32[272,128]{1,0:T(8,128)S(1)}, f32[128,128]{1,0:T(8,128)S(1)}, f32[399,128]{1,0:T(8,128)S(1)}, s32[]{:T(128)}, /*index=5*/s32[]{:T...) while((s32[]{:T(128)}, f32[272,128]{1,0:T(8,128)S(1)}, ...), condition=%wide.region_4.5_spmd.clone, body=%wide.region_3.4_spmd.clone.sunk | while | flops 591923 | bytes 1405823 | solution.py:51
  137.4 0.2 fusion.54
  137.7 0.2 fusion.54
  138.1 0.2 fusion.54
  138.4 0.2 fusion.54
  138.8 0.2 fusion.54
  139.1 0.2 fusion.54
  139.5 0.2 fusion.54
  139.9 0.2 fusion.54
  140.6 0.2 fusion.54
  140.9 0.2 fusion.54
  141.3 0.2 fusion.54
  142.0 0.2 fusion.54
  142.3 0.2 fusion.54
  142.7 0.2 fusion.54
  143.0 5.8 %while.33 = (s32[]{:T(128)}, f32[272,128]{1,0:T(8,128)S(1)}, f32[128,128]{1,0:T(8,128)S(1)}, f32[399,128]{1,0:T(8,128)S(1)}, s32[]{:T(128)}, /*index=5*/s32[]{:T...) while((s32[]{:T(128)}, f32[272,128]{1,0:T(8,128)S(1)}, ...), condition=%wide.region_2.3_spmd.clone, body=%wide.region_1.2_spmd.clone.sunk | while | flops 591939 | bytes 1405943 | solution.py:51
  143.2 0.2 fusion.52
  143.9 0.2 fusion.52
  144.2 0.2 fusion.52
  144.6 0.2 fusion.52
  145.3 0.2 fusion.52
  145.7 0.2 fusion.52
  146.0 0.2 fusion.52
  146.8 0.2 fusion.52
  147.1 0.2 fusion.52
  147.5 0.2 fusion.52
  148.2 0.2 fusion.52
  148.6 0.2 fusion.52
  148.8 3.1 %collective-permute-start.3 = (f32[2,3,128]{2,0,1:T(2,128)S(1)}, f32[2,3,128]{2,0,1:T(2,128)S(1)}, u32[]{:S(2)}, u32[]{:S(2)}) collective-permute-start(f32[2,3,128]{2,0,1:T(2,128)S(1)} %slice.73), channel_id=1, source_target_pairs={{2,0},{4,2},{6,4},{8,6},{10,8},{12,10},{14,12},{3,1},{5,3},{7,5},{... | collective-permute-start | bytes 9224 | tf_op jit(solution)/shard_map/ppermute | solution.py:13
  151.9 2.7 %convert_element_type.14 = f32[272,4096]{1,0:T(8,128)} convert(bf16[272,4096]{1,0:T(8,128)(2,1)S(1)} %copy-done) | non-fusion elementwise | flops 1114112 | bytes 6684672 | tf_op jit(solution)/shard_map/convert_element_type | solution.py:90
  154.6 3.0 %gather_fusion.1 = f32[16,4096]{1,0:T(8,128)S(1)} fusion(f32[272,4096]{1,0:T(8,128)} %convert_element_type.14, s32[1024]{0:T(1024)S(1)} %pad_clamp_fusion), kind=kCustom, calls=%fused_computation.1.clone | custom fusion | bytes 524352 | tf_op jit(solution)/shard_map/jit(_take)/gather | solution.py:94
  157.8 4.1 %all_gather.8 = bf16[272,3,256]{2,0,1:T(8,128)(2,1)S(1)} all-gather(bf16[272,3,128]{2,0,1:T(8,128)(2,1)S(1)} %fusion.37), channel_id=1, replica_groups=mesh['rep'=2,'seq'=8,'grp'=2] {'grp'}, dimensions={2}, use_global_device_ids=true | all-gather | bytes 626688 | tf_op jit(solution)/shard_map/all_gather | solution.py:85
  162.0 7.0 %multiply_reduce_fusion = (f32[272]{0:T(512)S(1)}, f32[272,4096]{1,0:T(8,128)}) fusion(bf16[272,4096]{1,0:T(8,128)(2,1)S(1)} %copy-done, bf16[272,3,256]{2,0,1:T(8,128)(2,1)S(1)} %all_gather.8, bf16[3,256,4096]{2,1,0:T(8,128)(2,1)} %all-gather.2.cloned.1.call-done), kind=kOutput, calls=%fused_computation.51 | convolution fusion | flops 1714618112 | bytes 13395008 | tf_op jit(solution)/shard_map/tfc,fcd->td/dot_general | solution.py:87
  169.0 3.0 %gather_fusion = f32[16,4096]{1,0:T(8,128)S(1)} fusion(f32[272,4096]{1,0:T(8,128)} %get-tuple-element.361, s32[1024]{0:T(1024)S(1)} %pad_clamp_fusion), kind=kCustom, calls=%fused_computation.clone | custom fusion | bytes 524352 | tf_op jit(solution)/shard_map/jit(_take)/gather | solution.py:93
  172.0 0.2 fusion.41
  172.2 2.5 %all-reduce = (f32[272]{0:T(512)S(1)}, f32[16]{0:T(128)S(1)}) all-reduce(f32[272]{0:T(512)S(1)} %get-tuple-element.360, f32[16]{0:T(128)S(1)} %fusion.41), channel_id=1, replica_groups=mesh['rep'=2,'seq'=8,'grp'=2] {'grp'}, use_global_device_ids=true, to_apply=%region_6.7 | all-reduce | flops 288 | bytes 2304 | tf_op jit(solution)/shard_map/psum | solution.py:97
  174.7 0.6 broadcast_multiply_fusion
  175.3 0.5 broadcast_multiply_fusion.1
  (74 shorter events, 2.6 us)
Async XLA Ops:
  7.2 100.9 %all-gather.2.cloned.1.call-start = ((), (), s32[]{:S(2)}) async-start(), calls=%async_computation.1 | async-start | bytes 7077888 | tf_op jit(solution)/shard_map/all_gather | solution.py:63
  7.9 120.0 %copy-start.3 = (f32[3,3,128]{2,1,0:T(4,128)S(1)}, f32[3,3,128]{2,1,0:T(4,128)}, u32[]{:S(2)}) copy-start(f32[3,3,128]{2,1,0:T(4,128)} %param.15) | copy-start | bytes 13828
  7.9 123.7 %copy-start.1 = (bf16[272,128]{1,0:T(8,128)(2,1)S(1)}, bf16[272,128]{1,0:T(8,128)(2,1)}, u32[]{:S(2)}) copy-start(bf16[272,128]{1,0:T(8,128)(2,1)} %param.17) | copy-start | bytes 208900
  7.9 125.9 %copy-start.5 = (s32[16]{0:T(128)S(1)}, s32[16]{0:T(128)}, u32[]{:S(2)}) copy-start(s32[16]{0:T(128)} %param.18) | copy-start | bytes 196
  7.9 126.0 %copy-start.4 = (f32[8,128]{1,0:T(8,128)S(1)}, f32[8,128]{1,0:T(8,128)}, u32[]{:S(2)}) copy-start(f32[8,128]{1,0:T(8,128)} %param.16) | copy-start | bytes 12292
  7.9 116.2 %reduce-scatter.2.cloned.1.call-start = ((), (), s32[]{:S(2)}) async-start(), calls=%async_computation.2 | async-start | bytes 1253376 | tf_op jit(solution)/shard_map/reduce_scatter | solution.py:66
  124.9 5.2 %collective-permute-start = (f32[2,3,128]{2,0,1:T(2,128)S(1)}, f32[2,3,128]{2,0,1:T(2,128)S(1)}, u32[]{:S(2)}, u32[]{:S(2)}) collective-permute-start(f32[2,3,128]{2,0,1:T(2,128)S(1)} %slice.65), channel_id=1, source_target_pairs={{0,2},{2,4},{4,6},{6,8},{8,10},{10,12},{12,14},{1,3},{3,5},{5,7},{... | collective-permute-start | bytes 9224 | tf_op jit(solution)/shard_map/ppermute | solution.py:13
  131.7 5.5 %collective-permute-start.2 = (f32[127,128]{1,0:T(8,128)S(1)}, f32[127,128]{1,0:T(8,128)S(1)}, u32[]{:S(2)}, u32[]{:S(2)}) collective-permute-start(f32[127,128]{1,0:T(8,128)S(1)} %slice.72), channel_id=1, source_target_pairs={{2,0},{4,2},{6,4},{8,6},{10,8},{12,10},{14,12},{3,1},{5,3},{7,5},{... | collective-permute-start | bytes 195080 | tf_op jit(solution)/shard_map/ppermute | solution.py:13
  134.0 8.9 %collective-permute-start.1 = (f32[127,128]{1,0:T(8,128)S(1)}, f32[127,128]{1,0:T(8,128)S(1)}, u32[]{:S(2)}, u32[]{:S(2)}) collective-permute-start(f32[127,128]{1,0:T(8,128)S(1)} %slice.70), channel_id=1, source_target_pairs={{0,2},{2,4},{4,6},{6,8},{8,10},{10,12},{12,14},{1,3},{3,5},{5,7},{... | collective-permute-start | bytes 195080 | tf_op jit(solution)/shard_map/ppermute | solution.py:13
  143.0 9.0 %copy-start = (bf16[272,4096]{1,0:T(8,128)(2,1)S(1)}, bf16[272,4096]{1,0:T(8,128)(2,1)}, u32[]{:S(2)}) copy-start(bf16[272,4096]{1,0:T(8,128)(2,1)} %param.13) | copy-start | bytes 6684676
  148.8 8.8 %collective-permute-start.3 = (f32[2,3,128]{2,0,1:T(2,128)S(1)}, f32[2,3,128]{2,0,1:T(2,128)S(1)}, u32[]{:S(2)}, u32[]{:S(2)}) collective-permute-start(f32[2,3,128]{2,0,1:T(2,128)S(1)} %slice.73), channel_id=1, source_target_pairs={{2,0},{4,2},{6,4},{8,6},{10,8},{12,10},{14,12},{3,1},{5,3},{7,5},{... | collective-permute-start | bytes 9224 | tf_op jit(solution)/shard_map/ppermute | solution.py:13
  162.0 10.0 %copy-start.2 = (bf16[16,4096]{1,0:T(8,128)(2,1)S(1)}, bf16[16,4096]{1,0:T(8,128)(2,1)}, u32[]{:S(2)}) copy-start(bf16[16,4096]{1,0:T(8,128)(2,1)} %param.19) | copy-start | bytes 393220
Sparse Core Ops, SparseCore 0:
  10.2 97.8 all-gather.1
  114.6 9.5 reduce-scatter.1
where the time goes:
time: 183 us
  waiting for transfers between devices  113 us (62%)
  between operations  14.3 us (8%)
  matrix products  13.3 us (7%)
  other arithmetic  11.7 us (6%)
  starting transfers between devices  11.5 us (6%)
  local copies, waits for them, and re-layouts  7.86 us (4%)
  blocking collectives  6.62 us (4%)
  loops' own time  4.69 us (3%)
    all_gather x1, waiting for transfers between devices, per_device(): lax.all_gather(proj, 'seq', axis=1, tiled=True)  100 us
    ppermute x4, starting transfers between devices, shifted(): return lax.ppermute(block, axis, route)  11.4 us
    reduce_scatter x1, waiting for transfers between devices, per_device(): lax.psum_scatter(partial_feature, 'grp', scatter_dimension=2, tiled=True)  9.68 us
    dot_general x1, matrix products, per_device(): jnp.einsum('tfc,fcd->td', all_channels, panels_again, preferred_element_t...  7 us
    dot_general x1, matrix products, per_device(): jnp.einsum('td,fcd->tfc', hidden, lax.all_gather(proj, 'seq', axis=1, til...  6.32 us
    add x32, other arithmetic, accumulate(): summed + lax.dynamic_index_in_dim(per_channel, offset, 0, keepdims=False)...  5.8 us
    another operation x2, loops' own time, long_filter(): lax.fori_loop(0, filter_span // 8, accumulate, jnp.zeros((row_count, exte...  4.69 us
    all_gather x1, blocking collectives, per_device(): all_channels = lax.all_gather(back_feature, 'grp', axis=2, tiled=True)  4.13 us
  transfers between devices with their start and end apart: 6, of which 3 were waited for; matrix products, arithmetic and copies ran while one was open for 5% of the time, Pallas kernels for 0%

commit v1 on v0

--- a/solution.py
+++ b/solution.py
@@ -5,6 +5,22 @@
 
 D = 8192
 GROUP = 16
+
+
+def ring_gather(x, axis, dim):
+    ways, here, step = (lax.axis_size(axis), lax.axis_index(axis), x.shape[dim])
+    dims = [n * ways if d == dim else n for d, n in enumerate(x.shape)]
+    full = lax.dynamic_update_slice_in_dim(jnp.zeros(dims, x.dtype), x, here * step, axis=dim)
+    going_up = going_down = x
+    for far in range(1, ways // 2 + 1):
+        going_up = lax.ppermute(going_up, axis, [(d, (d + 1) % ways) for d in range(ways)])
+        full = lax.dynamic_update_slice_in_dim(full, going_up, (here - far) % ways * step, axis=dim)
+        if 2 * far < ways:
+            going_down = lax.ppermute(going_down, axis, [(d, (d - 1) % ways) for d in range(ways)])
+            full = lax.dynamic_update_slice_in_dim(
+                full, going_down, (here + far) % ways * step, axis=dim
+            )
+    return full
 
 
 def shifted(block, axis, distance):
@@ -58,10 +74,7 @@
     tap_count = short_taps.shape[0]
     filter_span = filters.shape[1]
     partial_feature = jnp.einsum(
-        "td,fcd->tfc",
-        hidden,
-        lax.all_gather(proj, "seq", axis=1, tiled=True),
-        preferred_element_type=jnp.float32,
+        "td,fcd->tfc", hidden, ring_gather(proj, "seq", 1), preferred_element_type=jnp.float32
     )
     feature = lax.psum_scatter(partial_feature, "grp", scatter_dimension=2, tiled=True)
     short_rim = shifted(feature[row_count - tap_count + 1 :], "seq", 1)

time: 183 us -> 263 us (1.44); the launches traced: 183 us -> 259 us
  local copies, waits for them, and re-layouts: 7.86 us -> 42.9 us
  waiting for transfers between devices: 113 us -> 141 us
  starting transfers between devices: 11.5 us -> 23.9 us
  matrix products: 13.3 us -> 9.73 us
    ppermute x0 -> x7, waiting for transfers between devices: none -> 109 us  [the longest x4 108 us: ring_gather(): lax.ppermute(going_up, axis, [(d, (d + 1) % ways) for d in range(ways)])]
    all_gather x1, waiting for transfers between devices: 100 us -> 15.3 us  [per_device(): panels_again = lax.all_gather(proj, 'seq', axis=1, tiled=True)]
    mul x32, local copies, waits for them, and re-layouts: 0.99 us -> 31.8 us  [accumulate(): lax.dynamic_index_in_dim(per_channel, offset, 0, keepdims=False) * section]
    ppermute x0 -> x7, starting transfers between devices: none -> 8.92 us  [the longest x4 7.76 us: ring_gather(): lax.ppermute(going_up, axis, [(d, (d + 1) % ways) for d in range(ways)])]
    ppermute x4, starting transfers between devices: 11.4 us -> 14.9 us  [shifted(): return lax.ppermute(block, axis, route)]
    dot_general x1, matrix products: 6.32 us -> 2.86 us  [per_device(): jnp.einsum('td,fcd->tfc', hidden, ring_gather(proj, 'seq', 1), preferred_...]
    dynamic_update_slice x0 -> x8, local copies, waits for them, and re-layouts: none -> 2.81 us  [the longest x4 1.4 us: ring_gather(): lax.dynamic_update_slice_in_dim(full, going_up, (here - far) % ways * ste...]
    ppermute x4, waiting for transfers between devices: 2.14 us -> 4.86 us  [shifted(): return lax.ppermute(block, axis, route)]
  transfers between devices with their start and end apart: 6 -> 13, of which waited for: 3 -> 12; matrix products, arithmetic and copies ran while one was open for 5% -> 20% of each run, Pallas kernels for 0% -> 0%
where the time goes in v1:
time: 263 us; the launch traced here: 259 us
  waiting for transfers between devices  141 us (54%)
  local copies, waits for them, and re-layouts  42.9 us (16%)
  starting transfers between devices  23.9 us (9%)
  between operations  15.8 us (6%)
  other arithmetic  13 us (5%)
  matrix products  9.73 us (4%)
  blocking collectives  8.67 us (3%)
  loops' own time  3.62 us (1%)
    ppermute x4, waiting for transfers between devices, ring_gather(): lax.ppermute(going_up, axis, [(d, (d + 1) % ways) for d in range(ways)])  108 us
    mul x32, local copies, waits for them, and re-layouts, accumulate(): lax.dynamic_index_in_dim(per_channel, offset, 0, keepdims=False) * section  31.8 us
    all_gather x1, waiting for transfers between devices, per_device(): panels_again = lax.all_gather(proj, 'seq', axis=1, tiled=True)  15.3 us
    ppermute x4, starting transfers between devices, shifted(): return lax.ppermute(block, axis, route)  14.9 us
    reduce_scatter x1, waiting for transfers between devices, per_device(): lax.psum_scatter(partial_feature, 'grp', scatter_dimension=2, tiled=True)  11.2 us
    ppermute x4, starting transfers between devices, ring_gather(): lax.ppermute(going_up, axis, [(d, (d + 1) % ways) for d in range(ways)])  7.76 us
    dot_general x1, matrix products, per_device(): jnp.einsum('tfc,fcd->td', all_channels, panels_again, preferred_element_t...  6.87 us
    add x32, other arithmetic, accumulate(): summed + lax.dynamic_index_in_dim(per_channel, offset, 0, keepdims=False)...  5.79 us
  transfers between devices with their start and end apart: 13, of which 12 were waited for; matrix products, arithmetic and copies ran while one was open for 20% of the time, Pallas kernels for 0%

profile of v1, /device:TPU:9, one launch (start us, length us, event | category | flops | bytes accessed | tf_op | source)
XLA Modules:
  0.0 258.9 jit_solution(16569166137006766940)
XLA Ops:
  8.1 1.3 collective-permute-start
  9.3 1.2 collective-permute-start.1
  11.3 31.3 %collective-permute-done = bf16[3,32,4096]{2,1,0:T(8,128)(2,1)} collective-permute-done((bf16[3,32,4096]{2,1,0:T(8,128)(2,1)}, bf16[3,32,4096]{2,1,0:T(8,128)(2,1)}, u32[]{:S(2)}, u32[]{:S(2)}) %collective-permute-start) | collective-permute-done | bytes 786464 | tf_op jit(solution)/shard_map/ppermute | solution.py:16
  42.7 2.2 collective-permute-start.2
  45.6 1.2 constant_dynamic-update-slice_fusion.6
  46.8 1.2 constant_dynamic-update-slice_fusion.5
  48.1 29.4 %collective-permute-done.2 = bf16[3,32,4096]{2,1,0:T(8,128)(2,1)S(1)} collective-permute-done((bf16[3,32,4096]{2,1,0:T(8,128)(2,1)}, bf16[3,32,4096]{2,1,0:T(8,128)(2,1)S(1)}, u32[]{:S(2)}, u32[]{:S(2)}) %collective-permute-start.2) | collective-permute-done | bytes 786464 | tf_op jit(solution)/shard_map/ppermute | solution.py:16
  77.5 2.1 collective-permute-start.4
  80.3 31.8 %collective-permute-done.4 = bf16[3,32,4096]{2,1,0:T(8,128)(2,1)S(1)} collective-permute-done((bf16[3,32,4096]{2,1,0:T(8,128)(2,1)S(1)}, bf16[3,32,4096]{2,1,0:T(8,128)(2,1)S(1)}, u32[]{:S(2)}, u32[]{:S(2)}) %collective-permute-start.4) | collective-permute-done | bytes 786464 | tf_op jit(solution)/shard_map/ppermute | solution.py:16
  112.1 2.2 collective-permute-start.6
  114.8 15.1 %collective-permute-done.6 = bf16[3,32,4096]{2,1,0:T(8,128)(2,1)S(1)} collective-permute-done((bf16[3,32,4096]{2,1,0:T(8,128)(2,1)S(1)}, bf16[3,32,4096]{2,1,0:T(8,128)(2,1)S(1)}, u32[]{:S(2)}, u32[]{:S(2)}) %collective-permute-start.6) | collective-permute-done | bytes 786464 | tf_op jit(solution)/shard_map/ppermute | solution.py:16
  130.1 2.9 %fusion.32 = f32[272,3,256]{2,0,1:T(8,128)} fusion(bf16[3,256,4096]{2,1,0:T(8,128)(2,1)S(1)} %constant_dynamic-update-slice_fusion, bf16[272,4096]{1,0:T(8,128)(2,1)S(1)} %copy-done), kind=kOutput, calls=%fused_computation.54 | convolution fusion | flops 1711276032 | bytes 9355264 | tf_op jit(solution)/shard_map/td,fcd->tfc/dot_general | solution.py:76
  133.5 11.2 %reduce-scatter.2.cloned.1.call-done = f32[272,3,128]{2,0,1:T(8,128)} async-done(((f32[272,3,256]{2,0,1:T(8,128)}), f32[272,3,128]{2,0,1:T(8,128)}) %reduce-scatter.2.cloned.1.call-update) | async-done | bytes 417808 | tf_op jit(solution)/shard_map/reduce_scatter | solution.py:79
  145.4 3.1 %collective-permute-start.7 = (f32[2,3,128]{2,0,1:T(2,128)S(1)}, f32[2,3,128]{2,0,1:T(2,128)S(1)}, u32[]{:S(2)}, u32[]{:S(2)}) collective-permute-start(f32[2,3,128]{2,0,1:T(2,128)S(1)} %slice.65), channel_id=1, source_target_pairs={{0,2},{2,4},{4,6},{6,8},{8,10},{10,12},{12,14},{1,3},{3,5},{5,7},{... | collective-permute-start | bytes 9224 | tf_op jit(solution)/shard_map/ppermute | solution.py:29
  148.6 2.2 collective-permute-done.7
  150.8 1.5 fusion.38
  152.3 2.5 collective-permute-start.8
  156.1 3.7 %collective-permute-start.9 = (f32[127,128]{1,0:T(8,128)S(1)}, f32[127,128]{1,0:T(8,128)S(1)}, u32[]{:S(2)}, u32[]{:S(2)}) collective-permute-start(f32[127,128]{1,0:T(8,128)S(1)} %slice.72), channel_id=1, source_target_pairs={{2,0},{4,2},{6,4},{8,6},{10,8},{12,10},{14,12},{3,1},{5,3},{7,5},{... | collective-permute-start | bytes 195080 | tf_op jit(solution)/shard_map/ppermute | solution.py:29
  160.9 2.4 collective-permute-done.9
  163.3 20.7 %while.33 = (s32[]{:T(128)}, f32[272,128]{1,0:T(8,128)S(1)}, f32[128,128]{1,0:T(8,128)}, f32[399,128]{1,0:T(8,128)S(1)}, s32[]{:T(128)}, /*index=5*/s32[]{:T(128...) while((s32[]{:T(128)}, f32[272,128]{1,0:T(8,128)S(1)}, ...), condition=%wide.region_2.3_spmd.clone, body=%wide.region_1.2_spmd.clone.sunk | while | flops 591939 | bytes 1405943 | solution.py:67
  164.7 1.0 fusion.54
  166.0 1.0 fusion.54
  167.3 1.0 fusion.54
  168.6 1.0 fusion.54
  171.2 1.0 fusion.54
  172.5 1.0 fusion.54
  173.8 1.0 fusion.54
  178.9 1.0 fusion.54
  181.5 1.0 fusion.54
  182.8 1.0 fusion.54
  184.1 20.5 %while.34 = (s32[]{:T(128)}, f32[272,128]{1,0:T(8,128)S(1)}, f32[128,128]{1,0:T(8,128)}, f32[399,128]{1,0:T(8,128)S(1)}, s32[]{:T(128)}, /*index=5*/s32[]{:T(128...) while((s32[]{:T(128)}, f32[272,128]{1,0:T(8,128)S(1)}, ...), condition=%wide.region_4.5_spmd.clone, body=%wide.region_3.4_spmd.clone.sunk | while | flops 591923 | bytes 1405823 | solution.py:67
  185.4 1.0 fusion.56
  186.7 1.0 fusion.56
  188.0 1.0 fusion.56
  191.8 1.0 fusion.56
  193.1 1.0 fusion.56
  194.4 1.0 fusion.56
  199.5 1.0 fusion.56
  202.1 1.0 fusion.56
  203.4 1.0 fusion.56
  204.7 5.7 %collective-permute-start.10 = (f32[2,3,128]{2,0,1:T(2,128)S(1)}, f32[2,3,128]{2,0,1:T(2,128)S(1)}, u32[]{:S(2)}, u32[]{:S(2)}) collective-permute-start(f32[2,3,128]{2,0,1:T(2,128)S(1)} %slice.73), channel_id=1, source_target_pairs={{2,0},{4,2},{6,4},{8,6},{10,8},{12,10},{14,12},{3,1},{5,3},{7,5},{... | collective-permute-start | bytes 9224 | tf_op jit(solution)/shard_map/ppermute | solution.py:29
  210.4 2.7 %convert_element_type.14 = f32[272,4096]{1,0:T(8,128)} convert(bf16[272,4096]{1,0:T(8,128)(2,1)S(1)} %copy-done) | non-fusion elementwise | flops 1114112 | bytes 6684672 | tf_op jit(solution)/shard_map/convert_element_type | solution.py:103
  213.0 3.0 %gather_fusion.1 = f32[16,4096]{1,0:T(8,128)S(1)} fusion(f32[272,4096]{1,0:T(8,128)} %convert_element_type.14, s32[1024]{0:T(1024)S(1)} %pad_clamp_fusion), kind=kCustom, calls=%fused_computation.1.clone | custom fusion | bytes 524352 | tf_op jit(solution)/shard_map/jit(_take)/gather | solution.py:107
  216.3 4.7 %all_gather.6 = bf16[272,3,256]{2,0,1:T(8,128)(2,1)S(1)} all-gather(bf16[272,3,128]{2,0,1:T(8,128)(2,1)S(1)} %fusion.40), channel_id=1, replica_groups=mesh['rep'=2,'seq'=8,'grp'=2] {'grp'}, dimensions={2}, use_global_device_ids=true | all-gather | bytes 626688 | tf_op jit(solution)/shard_map/all_gather | solution.py:98
  221.0 15.3 %all-gather.2.cloned.1.call-done = bf16[3,256,4096]{2,1,0:T(8,128)(2,1)} async-done(((bf16[3,32,4096]{2,1,0:T(8,128)(2,1)}), bf16[3,256,4096]{2,1,0:T(8,128)(2,1)}) %all-gather.2.cloned.1.call-update) | async-done | bytes 6291472 | tf_op jit(solution)/shard_map/all_gather | solution.py:99
  236.2 6.9 %multiply_reduce_fusion = (f32[272]{0:T(512)S(1)}, f32[272,4096]{1,0:T(8,128)}) fusion(bf16[272,4096]{1,0:T(8,128)(2,1)S(1)} %copy-done, bf16[272,3,256]{2,0,1:T(8,128)(2,1)S(1)} %all_gather.6, bf16[3,256,4096]{2,1,0:T(8,128)(2,1)} %all-gather.2.cloned.1.call-done), kind=kOutput, calls=%fused_computation.51 | convolution fusion | flops 1714618112 | bytes 13395008 | tf_op jit(solution)/shard_map/tfc,fcd->td/dot_general | solution.py:100
  243.1 3.0 %gather_fusion = f32[16,4096]{1,0:T(8,128)S(1)} fusion(f32[272,4096]{1,0:T(8,128)} %get-tuple-element.361, s32[1024]{0:T(1024)S(1)} %pad_clamp_fusion), kind=kCustom, calls=%fused_computation.clone | custom fusion | bytes 524352 | tf_op jit(solution)/shard_map/jit(_take)/gather | solution.py:106
  246.4 4.0 %all-reduce = (f32[272]{0:T(512)S(1)}, f32[16]{0:T(128)S(1)}) all-reduce(f32[272]{0:T(512)S(1)} %get-tuple-element.360, f32[16]{0:T(128)S(1)} %fusion.44), channel_id=1, replica_groups=mesh['rep'=2,'seq'=8,'grp'=2] {'grp'}, use_global_device_ids=true, to_apply=%region_6.7 | all-reduce | flops 288 | bytes 2304 | tf_op jit(solution)/shard_map/psum | solution.py:110
  (103 shorter events, 26.9 us)
Async XLA Ops:
  8.0 3.2 %copy-start.1 = (bf16[3,32,4096]{2,1,0:T(8,128)(2,1)S(1)}, bf16[3,32,4096]{2,1,0:T(8,128)(2,1)}, u32[]{:S(2)}) copy-start(bf16[3,32,4096]{2,1,0:T(8,128)(2,1)} %param.14) | copy-start | bytes 2359300
  8.0 136.7 %reduce-scatter.2.cloned.1.call-start = ((), (), s32[]{:S(2)}) async-start(), calls=%async_computation.1 | async-start | bytes 1253376 | tf_op jit(solution)/shard_map/reduce_scatter | solution.py:79
  8.1 34.6 %collective-permute-start = (bf16[3,32,4096]{2,1,0:T(8,128)(2,1)}, bf16[3,32,4096]{2,1,0:T(8,128)(2,1)}, u32[]{:S(2)}, u32[]{:S(2)}) collective-permute-start(bf16[3,32,4096]{2,1,0:T(8,128)(2,1)} %param.14), channel_id=1, source_target_pairs={{0,2},{2,4},{4,6},{6,8},{8,10},{10,12},{12,14},{14,0},{1,3},{3,5},... | collective-permute-start | bytes 2359304 | tf_op jit(solution)/shard_map/ppermute | solution.py:16
  9.3 36.3 %collective-permute-start.1 = (bf16[3,32,4096]{2,1,0:T(8,128)(2,1)}, bf16[3,32,4096]{2,1,0:T(8,128)(2,1)}, u32[]{:S(2)}, u32[]{:S(2)}) collective-permute-start(bf16[3,32,4096]{2,1,0:T(8,128)(2,1)} %param.14), channel_id=1, source_target_pairs={{0,14},{2,0},{4,2},{6,4},{8,6},{10,8},{12,10},{14,12},{1,15},{3,1}... | collective-permute-start | bytes 2359304 | tf_op jit(solution)/shard_map/ppermute | solution.py:19
  11.3 118.8 %copy-start = (bf16[272,4096]{1,0:T(8,128)(2,1)S(1)}, bf16[272,4096]{1,0:T(8,128)(2,1)}, u32[]{:S(2)}) copy-start(bf16[272,4096]{1,0:T(8,128)(2,1)} %param.13) | copy-start | bytes 6684676
  42.7 34.8 %collective-permute-start.2 = (bf16[3,32,4096]{2,1,0:T(8,128)(2,1)}, bf16[3,32,4096]{2,1,0:T(8,128)(2,1)S(1)}, u32[]{:S(2)}, u32[]{:S(2)}) collective-permute-start(bf16[3,32,4096]{2,1,0:T(8,128)(2,1)} %collective-permute-done), channel_id=1, source_target_pairs={{0,2},{2,4},{4,6},{6,8},{8,10},{10,12},{12,14},{14,0},{1,3},{3,5},... | collective-permute-start | bytes 2359304 | tf_op jit(solution)/shard_map/ppermute | solution.py:16
  45.6 34.5 %collective-permute-start.3 = (bf16[3,32,4096]{2,1,0:T(8,128)(2,1)}, bf16[3,32,4096]{2,1,0:T(8,128)(2,1)S(1)}, u32[]{:S(2)}, u32[]{:S(2)}) collective-permute-start(bf16[3,32,4096]{2,1,0:T(8,128)(2,1)} %collective-permute-done.1), channel_id=1, source_target_pairs={{0,14},{2,0},{4,2},{6,4},{8,6},{10,8},{12,10},{14,12},{1,15},{3,1}... | collective-permute-start | bytes 2359304 | tf_op jit(solution)/shard_map/ppermute | solution.py:19
  77.5 34.6 %collective-permute-start.4 = (bf16[3,32,4096]{2,1,0:T(8,128)(2,1)S(1)}, bf16[3,32,4096]{2,1,0:T(8,128)(2,1)S(1)}, u32[]{:S(2)}, u32[]{:S(2)}) collective-permute-start(bf16[3,32,4096]{2,1,0:T(8,128)(2,1)S(1)} %collective-permute-done.2), channel_id=1, source_target_pairs={{0,2},{2,4},{4,6},{6,8},{8,10},{10,12},{12,14},{14,0},{1,3},{3,5},... | collective-permute-start | bytes 2359304 | tf_op jit(solution)/shard_map/ppermute | solution.py:16
  80.1 34.6 %collective-permute-start.5 = (bf16[3,32,4096]{2,1,0:T(8,128)(2,1)S(1)}, bf16[3,32,4096]{2,1,0:T(8,128)(2,1)S(1)}, u32[]{:S(2)}, u32[]{:S(2)}) collective-permute-start(bf16[3,32,4096]{2,1,0:T(8,128)(2,1)S(1)} %collective-permute-done.3), channel_id=1, source_target_pairs={{0,14},{2,0},{4,2},{6,4},{8,6},{10,8},{12,10},{14,12},{1,15},{3,1}... | collective-permute-start | bytes 2359304 | tf_op jit(solution)/shard_map/ppermute | solution.py:19
  112.1 17.8 %collective-permute-start.6 = (bf16[3,32,4096]{2,1,0:T(8,128)(2,1)S(1)}, bf16[3,32,4096]{2,1,0:T(8,128)(2,1)S(1)}, u32[]{:S(2)}, u32[]{:S(2)}) collective-permute-start(bf16[3,32,4096]{2,1,0:T(8,128)(2,1)S(1)} %collective-permute-done.4), channel_id=1, source_target_pairs={{0,2},{2,4},{4,6},{6,8},{8,10},{10,12},{12,14},{14,0},{1,3},{3,5},... | collective-permute-start | bytes 2359304 | tf_op jit(solution)/shard_map/ppermute | solution.py:16
  130.0 18.5 %copy-start.4 = (f32[3,3,128]{2,1,0:T(4,128)S(1)}, f32[3,3,128]{2,1,0:T(4,128)}, u32[]{:S(2)}) copy-start(f32[3,3,128]{2,1,0:T(4,128)} %param.15) | copy-start | bytes 13828
  130.0 22.2 %copy-start.2 = (bf16[272,128]{1,0:T(8,128)(2,1)S(1)}, bf16[272,128]{1,0:T(8,128)(2,1)}, u32[]{:S(2)}) copy-start(bf16[272,128]{1,0:T(8,128)(2,1)} %param.17) | copy-start | bytes 208900
  130.0 24.8 %copy-start.8 = (s32[16]{0:T(128)S(1)}, s32[16]{0:T(128)}, u32[]{:S(2)}) copy-start(s32[16]{0:T(128)} %param.18) | copy-start | bytes 196
  130.0 25.4 %copy-start.5 = (f32[8,128]{1,0:T(8,128)S(1)}, f32[8,128]{1,0:T(8,128)}, u32[]{:S(2)}) copy-start(f32[8,128]{1,0:T(8,128)} %param.16) | copy-start | bytes 12292
  132.9 103.3 %all-gather.2.cloned.1.call-start = ((), (), s32[]{:S(2)}) async-start(), calls=%async_computation.2 | async-start | bytes 7077888 | tf_op jit(solution)/shard_map/all_gather | solution.py:99
  145.4 5.3 %collective-permute-start.7 = (f32[2,3,128]{2,0,1:T(2,128)S(1)}, f32[2,3,128]{2,0,1:T(2,128)S(1)}, u32[]{:S(2)}, u32[]{:S(2)}) collective-permute-start(f32[2,3,128]{2,0,1:T(2,128)S(1)} %slice.65), channel_id=1, source_target_pairs={{0,2},{2,4},{4,6},{6,8},{8,10},{10,12},{12,14},{1,3},{3,5},{5,7},{... | collective-permute-start | bytes 9224 | tf_op jit(solution)/shard_map/ppermute | solution.py:29
  152.3 7.8 %collective-permute-start.8 = (f32[127,128]{1,0:T(8,128)S(1)}, f32[127,128]{1,0:T(8,128)}, u32[]{:S(2)}, u32[]{:S(2)}) collective-permute-start(f32[127,128]{1,0:T(8,128)S(1)} %slice.70), channel_id=1, source_target_pairs={{0,2},{2,4},{4,6},{6,8},{8,10},{10,12},{12,14},{1,3},{3,5},{5,7},{... | collective-permute-start | bytes 195080 | tf_op jit(solution)/shard_map/ppermute | solution.py:29
  156.1 7.2 %collective-permute-start.9 = (f32[127,128]{1,0:T(8,128)S(1)}, f32[127,128]{1,0:T(8,128)S(1)}, u32[]{:S(2)}, u32[]{:S(2)}) collective-permute-start(f32[127,128]{1,0:T(8,128)S(1)} %slice.72), channel_id=1, source_target_pairs={{2,0},{4,2},{6,4},{8,6},{10,8},{12,10},{14,12},{3,1},{5,3},{7,5},{... | collective-permute-start | bytes 195080 | tf_op jit(solution)/shard_map/ppermute | solution.py:29
  184.0 26.3 %copy-start.7 = (s32[16]{0:T(128)S(1)}, s32[16]{0:T(128)}, u32[]{:S(2)}) copy-start(s32[16]{0:T(128)} %get-tuple-element.336) | copy-start | bytes 196
  204.7 11.4 %collective-permute-start.10 = (f32[2,3,128]{2,0,1:T(2,128)S(1)}, f32[2,3,128]{2,0,1:T(2,128)S(1)}, u32[]{:S(2)}, u32[]{:S(2)}) collective-permute-start(f32[2,3,128]{2,0,1:T(2,128)S(1)} %slice.73), channel_id=1, source_target_pairs={{2,0},{4,2},{6,4},{8,6},{10,8},{12,10},{14,12},{3,1},{5,3},{7,5},{... | collective-permute-start | bytes 9224 | tf_op jit(solution)/shard_map/ppermute | solution.py:29
  221.0 25.2 %copy-start.3 = (bf16[16,4096]{1,0:T(8,128)(2,1)S(1)}, bf16[16,4096]{1,0:T(8,128)(2,1)}, u32[]{:S(2)}) copy-start(bf16[16,4096]{1,0:T(8,128)(2,1)} %param.19) | copy-start | bytes 393220
  221.0 25.2 %copy-start.6 = (pred[16]{0:T(512)(128)(4,1)S(1)}, pred[16]{0:T(512)(128)(4,1)}, u32[]{:S(2)}) copy-start(pred[16]{0:T(512)(128)(4,1)} %get-tuple-element.335) | copy-start | bytes 52
Sparse Core Ops, SparseCore 0:
  133.1 11.6 reduce-scatter.1
Sparse Core Ops, SparseCore 1:
  135.8 100.4 all-gather.1
